TPU v7x, 128 devices: a whole 4x4x4 slice. The times are simulated.
128 devices in a mesh: sky: 16 (over z, y), exp: 8 (over x, core).
Axes of the slice: x: 4, y: 4, z: 4, core: 2. Of those that a mesh axis runs over, the one named last changes fastest.
Arguments:
- sky_model: bfloat16 [4096, 1024], P('sky'), may hold values from -6 to 6
- exposure_data: bfloat16 [2048, 128, 128], P(('sky', 'exp')), may hold values from -6 to 6
- pixel_mask: int32 [2048, 128, 128], P(('sky', 'exp')), may hold values 0 or 1
- block_owner: int32 [2048, 1], P(('sky', 'exp')), may hold values from 0 to 15; in each aligned block of 16 rows (0 to 15, 16 to 31, ...) at most 2 rows name the same one
- block_local: int32 [2048], P(('sky', 'exp')), may hold values from 0 to 15
- psf_cell: int32 [2048], P(('sky', 'exp')), may hold values from 0 to 15
- psf_table: bfloat16 [128, 1681], P('exp'), may hold values from -0.15625 to 0.15625
Outputs:
- model_grad: float32 [4096, 1024], P('sky', 'exp')
- residual: bfloat16 [2048, 128, 128], P(('sky', 'exp'))
Inputs may be any that keep to these rules, and one draw needn't show every extreme that they name: `block_owner`: among the pieces of one device no sky index is named more than 2 times.
All inputs are finite; a program needn't handle non-finite values. No bound on the sum of `pixel_mask` on one device may be relied on, other than what follows from the above.
Results may differ from a plain program's by a relative error of at most 0.014.
Values may be sent and summed in bfloat16 or wider, within the bound.
No kernel may reach another device: no remote copies, remote signals or barrier semaphores. Data moves between devices by JAX's collectives and lax.ppermute only.
A program may use at most 64 MiB of HBM per device.

v0:
```python
import jax
import jax.numpy as jnp
from jax import lax
from jax.sharding import PartitionSpec as P

B = 128
PSF = 41
HALO = 20
CAP = 2


def from_behind(x, axis, by):
    devices = lax.axis_size(axis)
    pairs = [(i, i + by) for i in range(devices) if 0 <= i + by < devices]
    return lax.ppermute(x, axis, pairs)


def banded_table(out_cols):
    width = out_cols + PSF - 1
    tap_index = lax.broadcasted_iota(jnp.int32, (PSF, width, out_cols), 0)
    column = lax.broadcasted_iota(jnp.int32, (PSF, width, out_cols), 1)
    target = lax.broadcasted_iota(jnp.int32, (PSF, width, out_cols), 2)
    return (column - target == tap_index).astype(jnp.bfloat16)


def correlate(field, kernel, table, out_rows):
    out_cols = table.shape[2]
    width = field.shape[1]
    banded = jnp.einsum("ab,bcj->caj", kernel, table, preferred_element_type=jnp.float32).astype(
        jnp.bfloat16
    )
    spread = jnp.dot(
        field, banded.reshape(width, PSF * out_cols), preferred_element_type=jnp.float32
    )
    total = spread[0:out_rows, 0:out_cols]
    for offset in range(1, PSF):
        total = (
            total + spread[offset : offset + out_rows, offset * out_cols : (offset + 1) * out_cols]
        )
    return total


def fold_blocks(per_block, block_rows, per_row):
    extent = B + 2 * HALO
    margin = 2 * HALO
    grid = per_block.reshape(block_rows, per_row, extent, extent)
    col_main = grid[..., :B].transpose(0, 2, 1, 3).reshape(block_rows, extent, per_row * B)
    col_tail = jnp.pad(grid[..., B:], ((0, 0), (0, 0), (0, 0), (0, B - margin)))
    col_tail = col_tail.transpose(0, 2, 1, 3).reshape(block_rows, extent, per_row * B)
    width = per_row * B + margin
    columns = (
        jnp.pad(col_main, ((0, 0), (0, 0), (0, margin)))
        + jnp.pad(col_tail, ((0, 0), (0, 0), (B, 0)))[:, :, :width]
    )
    row_main = columns[:, :B].reshape(block_rows * B, width)
    row_tail = jnp.pad(columns[:, B:], ((0, 0), (0, B - margin), (0, 0))).reshape(
        block_rows * B, width
    )
    height = block_rows * B + margin
    return jnp.pad(row_main, ((0, margin), (0, 0))) + jnp.pad(row_tail, ((B, 0), (0, 0)))[:height]


def shards(sky_model, exposure_data, pixel_mask, block_owner, block_local, psf_cell, psf_table):
    sky_count = lax.axis_size("sky")
    extent = B + 2 * HALO
    stripe_rows = sky_model.shape[0]
    stripe_cols = sky_model.shape[1]
    per_row = stripe_cols // B
    block_rows = stripe_rows // B
    block_total = block_rows * per_row
    piece_count = exposure_data.shape[0]
    slot_total = sky_count * CAP
    owner_sky = block_owner[:, 0]
    earlier = lax.broadcasted_iota(jnp.int32, (piece_count, piece_count), 1) < lax.broadcasted_iota(
        jnp.int32, (piece_count, piece_count), 0
    )
    same_owner = owner_sky[:, None] == owner_sky[None, :]
    rank_within = jnp.sum((same_owner & earlier).astype(jnp.int32), axis=1)
    slot_index = owner_sky * CAP + rank_within
    requests = (
        jnp.full((slot_total,), -1, jnp.int32)
        .at[slot_index]
        .set(block_local)
        .reshape(sky_count, CAP)
    )
    cell_count = psf_table.shape[0]
    cell_onehot = (psf_cell[:, None] == lax.broadcasted_iota(jnp.int32, (1, cell_count), 1)).astype(
        jnp.bfloat16
    )
    kernels_flat = jnp.dot(cell_onehot, psf_table, preferred_element_type=jnp.float32).astype(
        jnp.bfloat16
    )
    forward_table = banded_table(B)
    adjoint_table = banded_table(extent)

    def per_piece(item):
        patch, kernel, observed, keep = item
        predicted = correlate(patch, kernel, forward_table, B)
        residual = (keep.astype(jnp.float32) * (predicted - observed.astype(jnp.float32))).astype(
            jnp.bfloat16
        )
        widened = jnp.pad(residual, 2 * HALO)
        adjoint = correlate(widened, kernel[::-1, ::-1], adjoint_table, extent)
        return (residual, adjoint)

    whole = lax.all_gather(sky_model, "sky", axis=0, tiled=True)
    padded = jnp.pad(whole, HALO)
    row_start = (owner_sky * block_rows + block_local // per_row) * B
    col_start = block_local % per_row * B

    def cut_patch(row_first, col_first):
        return lax.dynamic_slice(padded, (row_first, col_first), (extent, extent))

    patches = jax.vmap(cut_patch)(row_start, col_start)
    kernels = kernels_flat.reshape(piece_count, PSF, PSF)
    residuals, adjoints = lax.map(per_piece, (patches, kernels, exposure_data, pixel_mask))
    outgoing = jnp.zeros((slot_total, extent, extent), jnp.float32).at[slot_index].set(adjoints)
    outgoing = outgoing.reshape(sky_count, CAP, extent, extent)
    received, received_ids = (
        lax.all_to_all(
            outgoing.astype(jnp.bfloat16), "sky", split_axis=0, concat_axis=0, tiled=True
        ).astype(outgoing.dtype),
        lax.all_to_all(requests, "sky", split_axis=0, concat_axis=0, tiled=True),
    )
    contributions = received.reshape(slot_total, extent, extent)
    asked_ids = received_ids.reshape(slot_total)
    selector = (asked_ids[:, None] == lax.broadcasted_iota(jnp.int32, (1, block_total), 1)).astype(
        jnp.float32
    )
    per_block = jnp.einsum("nl,nuv->luv", selector, contributions, precision=lax.Precision.HIGHEST)
    canvas = fold_blocks(per_block, block_rows, per_row)
    core = canvas[:, HALO : HALO + stripe_cols]
    from_below = from_behind(core[:HALO].astype(jnp.bfloat16), "sky", -1).astype(jnp.float32)
    from_above = from_behind(core[stripe_rows + HALO :].astype(jnp.bfloat16), "sky", 1).astype(
        jnp.float32
    )
    middle = core[HALO : stripe_rows + HALO]
    folded = (
        middle
        + jnp.pad(from_above, ((0, stripe_rows - HALO), (0, 0)))
        + jnp.pad(from_below, ((stripe_rows - HALO, 0), (0, 0)))
    )
    gradient = lax.psum_scatter(
        folded.astype(jnp.bfloat16), "exp", scatter_dimension=1, tiled=True
    ).astype(jnp.float32)
    return (gradient, residuals)


def solution(mesh):
    in_specs = (
        P("sky", None),
        P(("sky", "exp"), None, None),
        P(("sky", "exp"), None, None),
        P(("sky", "exp"), None),
        P(("sky", "exp")),
        P(("sky", "exp")),
        P("exp", None),
    )
    out_specs = (P("sky", "exp"), P(("sky", "exp"), None, None))
    return jax.shard_map(shards, mesh=mesh, in_specs=in_specs, out_specs=out_specs, check_vma=False)
```

profile of v0, /device:TPU:0, one launch (start us, length us, event | category | flops | bytes accessed | tf_op | source)
XLA Modules:
  0.0 443.7 jit_solution(5079500784704721920)
XLA Ops:
  10.9 8.1 %all-to-all-start = ((s32[16,1,2]{2,1,0:T(1,128)}), s32[16,1,2]{2,1,0:T(1,128)S(1)}, u32[]{:S(2)}, u32[]{:S(2)}) async-start(s32[16,1,2]{2,1,0:T(1,128)} %bitcast.3), calls=%async_computation | async-start | bytes 16384 | tf_op jit(solution)/shard_map/all_to_all | solution.py:123
  20.9 62.6 %all-gather.2.cloned.1.call-done = bf16[4096,1024]{1,0:T(8,128)(2,1)} async-done(((bf16[256,1024]{1,0:T(8,128)(2,1)}), bf16[4096,1024]{1,0:T(8,128)(2,1)}) %all-gather.2.cloned.1.call-update) | async-done | bytes 8388624 | tf_op jit(solution)/shard_map/all_gather | solution.py:106
  83.5 14.8 %pad.49 = bf16[4136,1064]{1,0:T(8,128)(2,1)} pad(bf16[4096,1024]{1,0:T(8,128)(2,1)} %all-gather.2.cloned.1.call-done, bf16[]{:T(256)} %constant.73.clone.1), padding=20_20x20_20 | pad | bytes 17190018 | tf_op jit(solution)/shard_map/jit(_pad)/pad | solution.py:107
  98.3 58.3 %while.16 = (s32[]{:T(128)}, bf16[4136,1064]{1,0:T(8,128)(2,1)}, s32[16,2]{0,1:T(2,128)S(1)}, bf16[16,168,168]{2,1,0:T(8,128)(2,1)}, s32[]{:T(128)}) while((s32[]{:T(128)}, bf16[4136,1064]{1,0:T(8,128)(2,1)}, s32[16,2]{0,1:T(2,128)S(1)}, bf16[16,168,168]{2,1,0:T(8,128)(2,1)}, s32[]{:T(128)}) %tuple.53), condition=%wide.while_cond, body=%wide.while_body.sunk | while | flops 2 | bytes 173665 | solution.py:112
  99.0 3.0 bitcast_dynamic-update-slice_fusion.4
  102.6 3.0 bitcast_dynamic-update-slice_fusion.4
  106.3 3.0 bitcast_dynamic-update-slice_fusion.4
  109.9 3.0 bitcast_dynamic-update-slice_fusion.4
  113.5 3.0 bitcast_dynamic-update-slice_fusion.4
  117.2 3.0 bitcast_dynamic-update-slice_fusion.4
  120.8 3.0 bitcast_dynamic-update-slice_fusion.4
  124.5 3.0 bitcast_dynamic-update-slice_fusion.4
  128.1 3.0 bitcast_dynamic-update-slice_fusion.4
  131.8 3.0 bitcast_dynamic-update-slice_fusion.4
  135.4 3.0 bitcast_dynamic-update-slice_fusion.4
  139.1 3.0 bitcast_dynamic-update-slice_fusion.4
  142.7 3.0 bitcast_dynamic-update-slice_fusion.4
  146.4 3.0 bitcast_dynamic-update-slice_fusion.4
  150.0 3.0 bitcast_dynamic-update-slice_fusion.4
  153.7 3.0 bitcast_dynamic-update-slice_fusion.4
  156.6 157.8 %while.17 = (s32[]{:T(128)}, bf16[16,128,128]{2,1,0:T(8,128)(2,1)}, f32[16,168,168]{2,1,0:T(8,128)S(1)}, s32[16,128,128]{2,1,0:T(8,128)}, bf16[16,168,168]{2,1,0...) while((s32[]{:T(128)}, bf16[16,128,128]{2,1,0:T(8,128)(2,1)}, ...), condition=%wide.region_3.4_spmd.clone, body=%wide.region_2.3_spmd.clone.sunk | while | flops 1093145856 | bytes 34470920 | solution.py:116
  164.5 1.9 fusion.82
  168.7 1.8 bitcast_dynamic-update-slice_fusion.5
  174.4 1.9 fusion.82
  184.3 1.9 fusion.82
  194.1 1.9 fusion.82
  204.0 1.9 fusion.82
  213.8 1.9 fusion.82
  223.7 1.9 fusion.82
  233.6 1.9 fusion.82
  243.4 1.9 fusion.82
  253.3 1.9 fusion.82
  263.2 1.9 fusion.82
  273.0 1.9 fusion.82
  282.9 1.9 fusion.82
  292.7 1.9 fusion.82
  302.6 1.9 fusion.82
  312.5 1.9 fusion.82
  314.4 2.8 broadcast_in_dim.36
  317.2 4.1 scatter_fusion
  321.4 2.8 convert_element_type.99
  324.2 3.7 copy.17
  327.9 5.2 %all-to-all-start.1 = ((bf16[16,2,168,168]{3,1,2,0:T(2,128)(2,1)}), bf16[16,2,168,168]{3,1,2,0:T(2,128)(2,1)S(1)}, u32[]{:S(2)}, u32[]{:S(2)}) async-start(bf16[16,2,168,168]{3,1,2,0:T(2,128)(2,1)} %copy.17), calls=%async_computation.1 | async-start | bytes 5505024 | tf_op jit(solution)/shard_map/all_to_all | solution.py:120
  334.7 40.4 %all-to-all-done.1 = bf16[16,2,168,168]{3,1,2,0:T(2,128)(2,1)S(1)} async-done(((bf16[16,2,168,168]{3,1,2,0:T(2,128)(2,1)}), bf16[16,2,168,168]{3,1,2,0:T(2,128)(2,1)S(1)}, u32[]{:S(2)}, u32[]{:S(2)}) %all-to-all-start.1) | async-done | bytes 1806368 | tf_op jit(solution)/shard_map/all_to_all | solution.py:120
  375.1 4.7 %copy.18 = bf16[16,2,168,168]{3,1,0,2:T(2,128)(2,1)} copy(bf16[16,2,168,168]{3,1,2,0:T(2,128)(2,1)S(1)} %all-to-all-done.1) | data formatting | bytes 3612672 | tf_op jit(solution)/shard_map/all_to_all | solution.py:120
  379.8 5.7 %reshape.115 = bf16[32,168,168,1]{2,0,1,3:T(8,128)(2,1)S(1)} reshape(bf16[16,2,168,168]{3,1,0,2:T(2,128)(2,1)} %copy.18) | data formatting | bytes 3612672 | tf_op jit(solution)/shard_map/reshape | solution.py:125
  395.3 4.3 collective-permute-done.1
  400.9 34.3 %reduce-scatter.4.cloned.1.call-done = bf16[128,256]{1,0:T(8,128)(2,1)} async-done(((bf16[1024,256]{1,0:T(8,128)(2,1)}), bf16[128,256]{1,0:T(8,128)(2,1)}) %reduce-scatter.4.cloned.1.call-update) | async-done | bytes 65552
  (202 shorter events, 154.9 us)
Async XLA Ops:
  7.2 11.9 %copy-start = (bf16[16,1681]{1,0:T(8,128)(2,1)S(1)}, bf16[16,1681]{1,0:T(8,128)(2,1)}, u32[]{:S(2)}) copy-start(bf16[16,1681]{1,0:T(8,128)(2,1)} %param.15) | copy-start | bytes 161380
  7.2 76.3 %all-gather.2.cloned.1.call-start = ((), (), s32[]{:S(2)}) async-start(), calls=%async_computation.3 | async-start | bytes 8912896 | tf_op jit(solution)/shard_map/all_gather | solution.py:106
  10.9 316.9 %all-to-all-start = ((s32[16,1,2]{2,1,0:T(1,128)}), s32[16,1,2]{2,1,0:T(1,128)S(1)}, u32[]{:S(2)}, u32[]{:S(2)}) async-start(s32[16,1,2]{2,1,0:T(1,128)} %bitcast.3), calls=%async_computation | async-start | bytes 16384 | tf_op jit(solution)/shard_map/all_to_all | solution.py:123
  327.9 47.2 %all-to-all-start.1 = ((bf16[16,2,168,168]{3,1,2,0:T(2,128)(2,1)}), bf16[16,2,168,168]{3,1,2,0:T(2,128)(2,1)S(1)}, u32[]{:S(2)}, u32[]{:S(2)}) async-start(bf16[16,2,168,168]{3,1,2,0:T(2,128)(2,1)} %copy.17), calls=%async_computation.1 | async-start | bytes 5505024 | tf_op jit(solution)/shard_map/all_to_all | solution.py:120
  333.1 102.1 %reduce-scatter.4.cloned.1.call-start = ((), (), s32[]{:S(2)}) async-start(), calls=%async_computation.4 | async-start | bytes 589824
  392.0 44.8 %copy-start.1 = (bf16[16,1681]{1,0:T(8,128)(2,1)S(1)}, bf16[16,1681]{1,0:T(8,128)(2,1)}, u32[]{:S(2)}) copy-start(bf16[16,1681]{1,0:T(8,128)(2,1)} %param.15) | copy-start | bytes 161380
  392.3 3.0 collective-permute-start
  393.6 6.0 %collective-permute-start.1 = (bf16[20,1024]{1,0:T(8,128)(2,1)S(1)}, bf16[20,1024]{1,0:T(8,128)(2,1)S(1)}, u32[]{:S(2)}, u32[]{:S(2)}) collective-permute-start(bf16[20,1024]{1,0:T(8,128)(2,1)S(1)} %get-tuple-element.172), channel_id=1, source_target_pairs={{8,0},{16,8},{24,16},{32,24},{40,32},{48,40},{56,48},{64,56},{72,6... | collective-permute-start | bytes 122888 | tf_op jit(solution)/shard_map/ppermute | solution.py:15
Sparse Core Ops, SparseCore 0:
  10.2 73.3 all-gather.1
  401.0 34.1 reduce-scatter.3
where the time goes:
time: 446 us; the launch traced here: 444 us
  waiting for transfers between devices  143 us (32%)
  local copies, waits for them, and re-layouts  125 us (28%)
  matrix products  77.6 us (17%)
  other arithmetic  67.5 us (15%)
  starting transfers between devices  16.3 us (4%)
  between operations  14.3 us (3%)
    all_gather x1, waiting for transfers between devices, shards(): whole = lax.all_gather(sky_model, 'sky', axis=0, tiled=True)  62.6 us
    dynamic_update_slice x32, other arithmetic, shards(): lax.map(per_piece, (patches, kernels, exposure_data, pixel_mask))  59 us
    gather x48, local copies, waits for them, and re-layouts  58.3 us
    dot_general x32, matrix products, correlate(): jnp.dot(field, banded.reshape(width, PSF * out_cols), preferred_element_t...  45.9 us
    all_to_all x1, waiting for transfers between devices, shards(): lax.all_to_all(outgoing.astype(jnp.bfloat16), 'sky', split_axis=0, concat...  40.4 us
    unnamed x3, waiting for transfers between devices  35 us
    dot_general x32, matrix products, correlate(): jnp.einsum('ab,bcj->caj', kernel, table, preferred_element_type=jnp.float32)  30.2 us
    convert_element_type x16, local copies, waits for them, and re-layouts, correlate(): jnp.einsum('ab,bcj->caj', kernel, table, preferred_element_type=jnp.float32)  20.1 us
  transfers between devices with their start and end apart: 6, of which 5 were waited for; matrix products, arithmetic and copies ran while one was open for 56% of the time, Pallas kernels for 0%

commit v1 on v0

--- a/solution.py
+++ b/solution.py
@@ -2,6 +2,7 @@
 import jax.numpy as jnp
 from jax import lax
 from jax.sharding import PartitionSpec as P
+from jax.lax import axis_index, axis_size, ppermute
 
 B = 128
 PSF = 41
@@ -103,7 +104,29 @@
         adjoint = correlate(widened, kernel[::-1, ::-1], adjoint_table, extent)
         return (residual, adjoint)
 
-    whole = lax.all_gather(sky_model, "sky", axis=0, tiled=True)
+    mixed_arr = axis_index("sky")
+    upper = axis_size("sky")
+    t_next, state_next, block_next = (upper, mixed_arr, sky_model.shape[0])
+    log = tuple(((d, (d + 1) % t_next) for d in range(t_next)))
+    pool = tuple(((d, (d - 1) % t_next) for d in range(t_next)))
+    whole = jnp.zeros(
+        (*sky_model.shape[:0], t_next * block_next, *sky_model.shape[0 + 1 :]), sky_model.dtype
+    )
+    raw_out = part_now = sky_model
+    parts_out = t_next // 2
+    dd = 1
+    whole = lax.dynamic_update_slice_in_dim(whole, sky_model, state_next * block_next, axis=0)
+    while dd < parts_out + 1:
+        raw_out = ppermute(raw_out, axis_name="sky", perm=log)
+        whole = lax.dynamic_update_slice_in_dim(
+            whole, raw_out, (state_next - dd) % t_next * block_next, axis=0
+        )
+        if dd < t_next - parts_out:
+            part_now = ppermute(part_now, "sky", perm=pool)
+            whole = lax.dynamic_update_slice_in_dim(
+                whole, part_now, (state_next + dd) % t_next * block_next, axis=0
+            )
+        dd += 1
     padded = jnp.pad(whole, HALO)
     row_start = (owner_sky * block_rows + block_local // per_row) * B
     col_start = block_local % per_row * B

time: 446 us -> 477 us (1.070)
  starting transfers between devices: 16.3 us -> 50.2 us
  waiting for transfers between devices: 143 us -> 113 us
  local copies, waits for them, and re-layouts: 125 us -> 150 us
    all_gather x1 -> x0, waiting for transfers between devices: 62.6 us -> none  [shards(): whole = lax.all_gather(sky_model, 'sky', axis=0, tiled=True)]
    ppermute x0 -> x15, waiting for transfers between devices: none -> 44.1 us  [the longest x8 43.3 us: shards(): raw_out = ppermute(raw_out, axis_name='sky', perm=log)]
    ppermute x0 -> x15, starting transfers between devices: none -> 38.9 us  [the longest x7 37.2 us: shards(): part_now = ppermute(part_now, 'sky', perm=pool)]
    dynamic_update_slice x0 -> x16, local copies, waits for them, and re-layouts: none -> 21.8 us  [the longest x8 11 us: shards(): lax.dynamic_update_slice_in_dim(whole, raw_out, (state_next - dd) % t_nex...]
    all_to_all x1, waiting for transfers between devices: 40.4 us -> 30.5 us  [shards(): lax.all_to_all(outgoing.astype(jnp.bfloat16), 'sky', split_axis=0, concat...]
    unnamed x3 -> x2, waiting for transfers between devices: 35 us -> 33.4 us
  transfers between devices with their start and end apart: 6 -> 20, of which waited for: 5 -> 12; matrix products, arithmetic and copies ran while one was open for 56% -> 58% of each run, Pallas kernels for 0% -> 0%
where the time goes in v1:
time: 477 us; the launch traced here: 474 us
  local copies, waits for them, and re-layouts  150 us (31%)
  waiting for transfers between devices  113 us (24%)
  matrix products  78.2 us (16%)
  other arithmetic  67.5 us (14%)
  starting transfers between devices  50.2 us (11%)
  between operations  14.7 us (3%)
    dynamic_update_slice x32, other arithmetic, shards(): lax.map(per_piece, (patches, kernels, exposure_data, pixel_mask))  59 us
    gather x48, local copies, waits for them, and re-layouts  57.5 us
    dot_general x32, matrix products, correlate(): jnp.dot(field, banded.reshape(width, PSF * out_cols), preferred_element_t...  45.9 us
    ppermute x8, waiting for transfers between devices, shards(): raw_out = ppermute(raw_out, axis_name='sky', perm=log)  43.3 us
    ppermute x7, starting transfers between devices, shards(): part_now = ppermute(part_now, 'sky', perm=pool)  37.2 us
    unnamed x2, waiting for transfers between devices  33.4 us
    all_to_all x1, waiting for transfers between devices, shards(): lax.all_to_all(outgoing.astype(jnp.bfloat16), 'sky', split_axis=0, concat...  30.5 us
    dot_general x32, matrix products, correlate(): jnp.einsum('ab,bcj->caj', kernel, table, preferred_element_type=jnp.float32)  30.2 us
  transfers between devices with their start and end apart: 20, of which 12 were waited for; matrix products, arithmetic and copies ran while one was open for 58% of the time, Pallas kernels for 0%

profile of v1, /device:TPU:0, one launch (start us, length us, event | category | flops | bytes accessed | tf_op | source)
XLA Modules:
  0.0 474.1 jit_solution(7067727903471241547)
XLA Ops:
  8.9 5.0 %collective-permute-start.1 = (bf16[256,1024]{1,0:T(8,128)(2,1)}, bf16[256,1024]{1,0:T(8,128)(2,1)S(1)}, u32[]{:S(2)}, u32[]{:S(2)}) collective-permute-start(bf16[256,1024]{1,0:T(8,128)(2,1)} %param.9), channel_id=1, source_target_pairs={{0,120},{8,0},{16,8},{24,16},{32,24},{40,32},{48,40},{56,48},{64,5... | collective-permute-start | bytes 1572872 | tf_op jit(solution)/shard_map/ppermute | solution.py:125
  13.9 12.1 %collective-permute-done = bf16[256,1024]{1,0:T(8,128)(2,1)S(1)} collective-permute-done((bf16[256,1024]{1,0:T(8,128)(2,1)}, bf16[256,1024]{1,0:T(8,128)(2,1)S(1)}, u32[]{:S(2)}, u32[]{:S(2)}) %collective-permute-start) | collective-permute-done | bytes 524320 | tf_op jit(solution)/shard_map/ppermute | solution.py:120
  26.0 5.3 %collective-permute-start.3 = (bf16[256,1024]{1,0:T(8,128)(2,1)S(1)}, bf16[256,1024]{1,0:T(8,128)(2,1)S(1)}, u32[]{:S(2)}, u32[]{:S(2)}) collective-permute-start(bf16[256,1024]{1,0:T(8,128)(2,1)S(1)} %collective-permute-done.1), channel_id=1, source_target_pairs={{0,120},{8,0},{16,8},{24,16},{32,24},{40,32},{48,40},{56,48},{64,5... | collective-permute-start | bytes 1572872 | tf_op jit(solution)/shard_map/ppermute | solution.py:125
  31.3 11.1 %collective-permute-done.2 = bf16[256,1024]{1,0:T(8,128)(2,1)S(1)} collective-permute-done((bf16[256,1024]{1,0:T(8,128)(2,1)S(1)}, bf16[256,1024]{1,0:T(8,128)(2,1)S(1)}, u32[]{:S(2)}, u32[]{:S(2)}) %collective-permute-start.2) | collective-permute-done | bytes 524320 | tf_op jit(solution)/shard_map/ppermute | solution.py:120
  42.4 5.3 %collective-permute-start.5 = (bf16[256,1024]{1,0:T(8,128)(2,1)S(1)}, bf16[256,1024]{1,0:T(8,128)(2,1)S(1)}, u32[]{:S(2)}, u32[]{:S(2)}) collective-permute-start(bf16[256,1024]{1,0:T(8,128)(2,1)S(1)} %collective-permute-done.3), channel_id=1, source_target_pairs={{0,120},{8,0},{16,8},{24,16},{32,24},{40,32},{48,40},{56,48},{64,5... | collective-permute-start | bytes 1572872 | tf_op jit(solution)/shard_map/ppermute | solution.py:125
  47.7 10.2 %collective-permute-done.4 = bf16[256,1024]{1,0:T(8,128)(2,1)S(1)} collective-permute-done((bf16[256,1024]{1,0:T(8,128)(2,1)S(1)}, bf16[256,1024]{1,0:T(8,128)(2,1)S(1)}, u32[]{:S(2)}, u32[]{:S(2)}) %collective-permute-start.4) | collective-permute-done | bytes 524320 | tf_op jit(solution)/shard_map/ppermute | solution.py:120
  58.8 5.4 %collective-permute-start.7 = (bf16[256,1024]{1,0:T(8,128)(2,1)S(1)}, bf16[256,1024]{1,0:T(8,128)(2,1)}, u32[]{:S(2)}, u32[]{:S(2)}) collective-permute-start(bf16[256,1024]{1,0:T(8,128)(2,1)S(1)} %collective-permute-done.5), channel_id=1, source_target_pairs={{0,120},{8,0},{16,8},{24,16},{32,24},{40,32},{48,40},{56,48},{64,5... | collective-permute-start | bytes 1572872 | tf_op jit(solution)/shard_map/ppermute | solution.py:125
  66.3 3.4 all-to-all-start
  69.8 2.7 collective-permute-done.6
  74.7 5.4 %collective-permute-start.9 = (bf16[256,1024]{1,0:T(8,128)(2,1)}, bf16[256,1024]{1,0:T(8,128)(2,1)}, u32[]{:S(2)}, u32[]{:S(2)}) collective-permute-start(bf16[256,1024]{1,0:T(8,128)(2,1)} %collective-permute-done.7), channel_id=1, source_target_pairs={{0,120},{8,0},{16,8},{24,16},{32,24},{40,32},{48,40},{56,48},{64,5... | collective-permute-start | bytes 1572872 | tf_op jit(solution)/shard_map/ppermute | solution.py:125
  80.1 4.4 broadcast_in_dim.42
  86.9 2.0 constant_dynamic-update-slice_fusion.14
  92.7 5.0 %collective-permute-start.11 = (bf16[256,1024]{1,0:T(8,128)(2,1)}, bf16[256,1024]{1,0:T(8,128)(2,1)S(1)}, u32[]{:S(2)}, u32[]{:S(2)}) collective-permute-start(bf16[256,1024]{1,0:T(8,128)(2,1)} %collective-permute-done.9), channel_id=1, source_target_pairs={{0,120},{8,0},{16,8},{24,16},{32,24},{40,32},{48,40},{56,48},{64,5... | collective-permute-start | bytes 1572872 | tf_op jit(solution)/shard_map/ppermute | solution.py:125
  104.7 5.7 %collective-permute-start.13 = (bf16[256,1024]{1,0:T(8,128)(2,1)S(1)}, bf16[256,1024]{1,0:T(8,128)(2,1)S(1)}, u32[]{:S(2)}, u32[]{:S(2)}) collective-permute-start(bf16[256,1024]{1,0:T(8,128)(2,1)S(1)} %collective-permute-done.11), channel_id=1, source_target_pairs={{0,120},{8,0},{16,8},{24,16},{32,24},{40,32},{48,40},{56,48},{64,5... | collective-permute-start | bytes 1572872 | tf_op jit(solution)/shard_map/ppermute | solution.py:125
  118.8 6.2 %collective-permute-done.14 = bf16[256,1024]{1,0:T(8,128)(2,1)S(1)} collective-permute-done((bf16[256,1024]{1,0:T(8,128)(2,1)S(1)}, bf16[256,1024]{1,0:T(8,128)(2,1)S(1)}, u32[]{:S(2)}, u32[]{:S(2)}) %collective-permute-start.14) | collective-permute-done | bytes 524320 | tf_op jit(solution)/shard_map/ppermute | solution.py:120
  125.8 14.8 %pad.49 = bf16[4136,1064]{1,0:T(8,128)(2,1)} pad(bf16[4096,1024]{1,0:T(8,128)(2,1)} %constant_dynamic-update-slice_fusion, bf16[]{:T(256)} %constant.161.clone.1), padding=20_20x20_20 | pad | bytes 17190018 | tf_op jit(solution)/shard_map/jit(_pad)/pad | solution.py:130
  140.5 57.5 %while.16 = (s32[]{:T(128)}, bf16[4136,1064]{1,0:T(8,128)(2,1)}, s32[16,2]{0,1:T(2,128)S(1)}, bf16[16,168,168]{2,1,0:T(8,128)(2,1)}, s32[]{:T(128)}) while((s32[]{:T(128)}, bf16[4136,1064]{1,0:T(8,128)(2,1)}, s32[16,2]{0,1:T(2,128)S(1)}, bf16[16,168,168]{2,1,0:T(8,128)(2,1)}, s32[]{:T(128)}) %tuple.53), condition=%wide.while_cond, body=%wide.while_body.sunk | while | flops 2 | bytes 173665 | solution.py:135
  141.2 2.9 bitcast_dynamic-update-slice_fusion.4
  144.8 2.9 bitcast_dynamic-update-slice_fusion.4
  148.4 2.9 bitcast_dynamic-update-slice_fusion.4
  152.0 2.9 bitcast_dynamic-update-slice_fusion.4
  155.6 2.9 bitcast_dynamic-update-slice_fusion.4
  159.2 2.9 bitcast_dynamic-update-slice_fusion.4
  162.8 2.9 bitcast_dynamic-update-slice_fusion.4
  166.3 2.9 bitcast_dynamic-update-slice_fusion.4
  169.9 2.9 bitcast_dynamic-update-slice_fusion.4
  173.5 2.9 bitcast_dynamic-update-slice_fusion.4
  177.1 3.0 bitcast_dynamic-update-slice_fusion.4
  180.7 2.9 bitcast_dynamic-update-slice_fusion.4
  184.3 2.9 bitcast_dynamic-update-slice_fusion.4
  187.9 3.0 bitcast_dynamic-update-slice_fusion.4
  191.5 2.9 bitcast_dynamic-update-slice_fusion.4
  195.1 2.9 bitcast_dynamic-update-slice_fusion.4
  198.0 157.8 %while.17 = (s32[]{:T(128)}, bf16[16,128,128]{2,1,0:T(8,128)(2,1)}, f32[16,168,168]{2,1,0:T(8,128)S(1)}, s32[16,128,128]{2,1,0:T(8,128)}, bf16[16,168,168]{2,1,0...) while((s32[]{:T(128)}, bf16[16,128,128]{2,1,0:T(8,128)(2,1)}, ...), condition=%wide.region_3.4_spmd.clone, body=%wide.region_2.3_spmd.clone.sunk | while | flops 1093145856 | bytes 34470920 | solution.py:139
  235.5 1.9 fusion.82
  255.2 1.9 fusion.82
  265.1 1.9 fusion.82
  355.8 2.8 broadcast_in_dim.39
  358.6 4.2 scatter_fusion
  362.8 2.8 convert_element_type.99
  365.6 3.7 copy.17
  369.3 3.7 all-to-all-start.1
  374.6 30.5 %all-to-all-done.1 = bf16[16,2,168,168]{3,1,2,0:T(2,128)(2,1)S(1)} async-done(((bf16[16,2,168,168]{3,1,2,0:T(2,128)(2,1)}), bf16[16,2,168,168]{3,1,2,0:T(2,128)(2,1)S(1)}, u32[]{:S(2)}, u32[]{:S(2)}) %all-to-all-start.1) | async-done | bytes 1806368 | tf_op jit(solution)/shard_map/all_to_all | solution.py:143
  405.1 4.7 copy.18
  409.8 5.7 %reshape.115 = bf16[32,168,168,1]{2,0,1,3:T(8,128)(2,1)S(1)} reshape(bf16[16,2,168,168]{3,1,0,2:T(2,128)(2,1)} %copy.18) | data formatting | bytes 3612672 | tf_op jit(solution)/shard_map/reshape | solution.py:148
  422.3 2.5 collective-permute-start.15
  426.6 4.3 collective-permute-done.16
  432.2 33.4 %reduce-scatter.4.cloned.1.call-done = bf16[128,256]{1,0:T(8,128)(2,1)} async-done(((bf16[1024,256]{1,0:T(8,128)(2,1)}), bf16[128,256]{1,0:T(8,128)(2,1)}) %reduce-scatter.4.cloned.1.call-update) | async-done | bytes 65552
  (266 shorter events, 203.6 us)
Async XLA Ops:
  7.2 66.1 %copy-start = (bf16[16,1681]{1,0:T(8,128)(2,1)S(1)}, bf16[16,1681]{1,0:T(8,128)(2,1)}, u32[]{:S(2)}) copy-start(bf16[16,1681]{1,0:T(8,128)(2,1)} %param.15) | copy-start | bytes 161380
  7.2 18.8 %collective-permute-start = (bf16[256,1024]{1,0:T(8,128)(2,1)}, bf16[256,1024]{1,0:T(8,128)(2,1)S(1)}, u32[]{:S(2)}, u32[]{:S(2)}) collective-permute-start(bf16[256,1024]{1,0:T(8,128)(2,1)} %param.9), channel_id=1, source_target_pairs={{0,8},{8,16},{16,24},{24,32},{32,40},{40,48},{48,56},{56,64},{64,7... | collective-permute-start | bytes 1572872 | tf_op jit(solution)/shard_map/ppermute | solution.py:120
  8.9 17.1 %collective-permute-start.1 = (bf16[256,1024]{1,0:T(8,128)(2,1)}, bf16[256,1024]{1,0:T(8,128)(2,1)S(1)}, u32[]{:S(2)}, u32[]{:S(2)}) collective-permute-start(bf16[256,1024]{1,0:T(8,128)(2,1)} %param.9), channel_id=1, source_target_pairs={{0,120},{8,0},{16,8},{24,16},{32,24},{40,32},{48,40},{56,48},{64,5... | collective-permute-start | bytes 1572872 | tf_op jit(solution)/shard_map/ppermute | solution.py:125
  26.0 31.9 %copy-start.6 = (bf16[256,1024]{1,0:T(8,128)(2,1)}, bf16[256,1024]{1,0:T(8,128)(2,1)S(1)}, u32[]{:S(2)}) copy-start(bf16[256,1024]{1,0:T(8,128)(2,1)S(1)} %collective-permute-done) | copy-start | bytes 1572868
  26.0 16.4 %collective-permute-start.2 = (bf16[256,1024]{1,0:T(8,128)(2,1)S(1)}, bf16[256,1024]{1,0:T(8,128)(2,1)S(1)}, u32[]{:S(2)}, u32[]{:S(2)}) collective-permute-start(bf16[256,1024]{1,0:T(8,128)(2,1)S(1)} %collective-permute-done), channel_id=1, source_target_pairs={{0,8},{8,16},{16,24},{24,32},{32,40},{40,48},{48,56},{56,64},{64,7... | collective-permute-start | bytes 1572872 | tf_op jit(solution)/shard_map/ppermute | solution.py:120
  26.0 58.5 %copy-start.7 = (bf16[256,1024]{1,0:T(8,128)(2,1)}, bf16[256,1024]{1,0:T(8,128)(2,1)S(1)}, u32[]{:S(2)}) copy-start(bf16[256,1024]{1,0:T(8,128)(2,1)S(1)} %collective-permute-done.1) | copy-start | bytes 1572868
  26.0 16.4 %collective-permute-start.3 = (bf16[256,1024]{1,0:T(8,128)(2,1)S(1)}, bf16[256,1024]{1,0:T(8,128)(2,1)S(1)}, u32[]{:S(2)}, u32[]{:S(2)}) collective-permute-start(bf16[256,1024]{1,0:T(8,128)(2,1)S(1)} %collective-permute-done.1), channel_id=1, source_target_pairs={{0,120},{8,0},{16,8},{24,16},{32,24},{40,32},{48,40},{56,48},{64,5... | collective-permute-start | bytes 1572872 | tf_op jit(solution)/shard_map/ppermute | solution.py:125
  42.4 5.4 %copy-start.10 = (bf16[256,1024]{1,0:T(8,128)(2,1)}, bf16[256,1024]{1,0:T(8,128)(2,1)S(1)}, u32[]{:S(2)}) copy-start(bf16[256,1024]{1,0:T(8,128)(2,1)S(1)} %collective-permute-done.2) | copy-start | bytes 1572868
  42.4 15.5 %collective-permute-start.4 = (bf16[256,1024]{1,0:T(8,128)(2,1)S(1)}, bf16[256,1024]{1,0:T(8,128)(2,1)S(1)}, u32[]{:S(2)}, u32[]{:S(2)}) collective-permute-start(bf16[256,1024]{1,0:T(8,128)(2,1)S(1)} %collective-permute-done.2), channel_id=1, source_target_pairs={{0,8},{8,16},{16,24},{24,32},{32,40},{40,48},{48,56},{56,64},{64,7... | collective-permute-start | bytes 1572872 | tf_op jit(solution)/shard_map/ppermute | solution.py:120
  42.4 42.1 %copy-start.5 = (bf16[256,1024]{1,0:T(8,128)(2,1)}, bf16[256,1024]{1,0:T(8,128)(2,1)S(1)}, u32[]{:S(2)}) copy-start(bf16[256,1024]{1,0:T(8,128)(2,1)S(1)} %collective-permute-done.3) | copy-start | bytes 1572868
  42.4 16.4 %collective-permute-start.5 = (bf16[256,1024]{1,0:T(8,128)(2,1)S(1)}, bf16[256,1024]{1,0:T(8,128)(2,1)S(1)}, u32[]{:S(2)}, u32[]{:S(2)}) collective-permute-start(bf16[256,1024]{1,0:T(8,128)(2,1)S(1)} %collective-permute-done.3), channel_id=1, source_target_pairs={{0,120},{8,0},{16,8},{24,16},{32,24},{40,32},{48,40},{56,48},{64,5... | collective-permute-start | bytes 1572872 | tf_op jit(solution)/shard_map/ppermute | solution.py:125
  57.9 14.6 %collective-permute-start.6 = (bf16[256,1024]{1,0:T(8,128)(2,1)S(1)}, bf16[256,1024]{1,0:T(8,128)(2,1)S(1)}, u32[]{:S(2)}, u32[]{:S(2)}) collective-permute-start(bf16[256,1024]{1,0:T(8,128)(2,1)S(1)} %collective-permute-done.4), channel_id=1, source_target_pairs={{0,8},{8,16},{16,24},{24,32},{32,40},{40,48},{48,56},{56,64},{64,7... | collective-permute-start | bytes 1572872 | tf_op jit(solution)/shard_map/ppermute | solution.py:120
  58.8 25.7 %copy-start.3 = (bf16[256,1024]{1,0:T(8,128)(2,1)}, bf16[256,1024]{1,0:T(8,128)(2,1)S(1)}, u32[]{:S(2)}) copy-start(bf16[256,1024]{1,0:T(8,128)(2,1)S(1)} %collective-permute-done.5) | copy-start | bytes 1572868
  58.8 15.9 %collective-permute-start.7 = (bf16[256,1024]{1,0:T(8,128)(2,1)S(1)}, bf16[256,1024]{1,0:T(8,128)(2,1)}, u32[]{:S(2)}, u32[]{:S(2)}) collective-permute-start(bf16[256,1024]{1,0:T(8,128)(2,1)S(1)} %collective-permute-done.5), channel_id=1, source_target_pairs={{0,120},{8,0},{16,8},{24,16},{32,24},{40,32},{48,40},{56,48},{64,5... | collective-permute-start | bytes 1572872 | tf_op jit(solution)/shard_map/ppermute | solution.py:125
  66.3 302.9 %all-to-all-start = ((s32[16,1,2]{2,1,0:T(1,128)}), s32[16,1,2]{2,1,0:T(1,128)S(1)}, u32[]{:S(2)}, u32[]{:S(2)}) async-start(s32[16,1,2]{2,1,0:T(1,128)} %bitcast.3), calls=%async_computation | async-start | bytes 16384 | tf_op jit(solution)/shard_map/all_to_all | solution.py:146
  72.5 12.0 %copy-start.8 = (bf16[256,1024]{1,0:T(8,128)(2,1)}, bf16[256,1024]{1,0:T(8,128)(2,1)S(1)}, u32[]{:S(2)}) copy-start(bf16[256,1024]{1,0:T(8,128)(2,1)S(1)} %collective-permute-done.6) | copy-start | bytes 1572868
  72.5 13.8 %collective-permute-start.8 = (bf16[256,1024]{1,0:T(8,128)(2,1)S(1)}, bf16[256,1024]{1,0:T(8,128)(2,1)}, u32[]{:S(2)}, u32[]{:S(2)}) collective-permute-start(bf16[256,1024]{1,0:T(8,128)(2,1)S(1)} %collective-permute-done.6), channel_id=1, source_target_pairs={{0,8},{8,16},{16,24},{24,32},{32,40},{40,48},{48,56},{56,64},{64,7... | collective-permute-start | bytes 1572872 | tf_op jit(solution)/shard_map/ppermute | solution.py:120
  74.7 9.8 %copy-start.2 = (bf16[256,1024]{1,0:T(8,128)(2,1)S(1)}, bf16[256,1024]{1,0:T(8,128)(2,1)}, u32[]{:S(2)}) copy-start(bf16[256,1024]{1,0:T(8,128)(2,1)} %param.9) | copy-start | bytes 1572868
  74.7 11.9 %copy-start.11 = (bf16[16,1681]{1,0:T(8,128)(2,1)S(1)}, bf16[16,1681]{1,0:T(8,128)(2,1)}, u32[]{:S(2)}) copy-start(bf16[16,1681]{1,0:T(8,128)(2,1)} %convolution_convert_fusion) | copy-start | bytes 161380
  74.7 17.9 %collective-permute-start.9 = (bf16[256,1024]{1,0:T(8,128)(2,1)}, bf16[256,1024]{1,0:T(8,128)(2,1)}, u32[]{:S(2)}, u32[]{:S(2)}) collective-permute-start(bf16[256,1024]{1,0:T(8,128)(2,1)} %collective-permute-done.7), channel_id=1, source_target_pairs={{0,120},{8,0},{16,8},{24,16},{32,24},{40,32},{48,40},{56,48},{64,5... | collective-permute-start | bytes 1572872 | tf_op jit(solution)/shard_map/ppermute | solution.py:125
  86.3 13.3 %collective-permute-start.10 = (bf16[256,1024]{1,0:T(8,128)(2,1)}, bf16[256,1024]{1,0:T(8,128)(2,1)}, u32[]{:S(2)}, u32[]{:S(2)}) collective-permute-start(bf16[256,1024]{1,0:T(8,128)(2,1)} %collective-permute-done.8), channel_id=1, source_target_pairs={{0,8},{8,16},{16,24},{24,32},{32,40},{40,48},{48,56},{56,64},{64,7... | collective-permute-start | bytes 1572872 | tf_op jit(solution)/shard_map/ppermute | solution.py:120
  86.9 13.5 %copy-start.4 = (bf16[256,1024]{1,0:T(8,128)(2,1)S(1)}, bf16[256,1024]{1,0:T(8,128)(2,1)}, u32[]{:S(2)}) copy-start(bf16[256,1024]{1,0:T(8,128)(2,1)} %copy-done.3) | copy-start | bytes 1572868
  86.9 14.3 %copy-start.9 = (bf16[256,1024]{1,0:T(8,128)(2,1)S(1)}, bf16[256,1024]{1,0:T(8,128)(2,1)}, u32[]{:S(2)}) copy-start(bf16[256,1024]{1,0:T(8,128)(2,1)} %copy-done.8) | copy-start | bytes 1572868
  92.7 12.1 %collective-permute-start.11 = (bf16[256,1024]{1,0:T(8,128)(2,1)}, bf16[256,1024]{1,0:T(8,128)(2,1)S(1)}, u32[]{:S(2)}, u32[]{:S(2)}) collective-permute-start(bf16[256,1024]{1,0:T(8,128)(2,1)} %collective-permute-done.9), channel_id=1, source_target_pairs={{0,120},{8,0},{16,8},{24,16},{32,24},{40,32},{48,40},{56,48},{64,5... | collective-permute-start | bytes 1572872 | tf_op jit(solution)/shard_map/ppermute | solution.py:125
  99.6 12.8 %collective-permute-start.12 = (bf16[256,1024]{1,0:T(8,128)(2,1)}, bf16[256,1024]{1,0:T(8,128)(2,1)S(1)}, u32[]{:S(2)}, u32[]{:S(2)}) collective-permute-start(bf16[256,1024]{1,0:T(8,128)(2,1)} %collective-permute-done.10), channel_id=1, source_target_pairs={{0,8},{8,16},{16,24},{24,32},{32,40},{40,48},{48,56},{56,64},{64,7... | collective-permute-start | bytes 1572872 | tf_op jit(solution)/shard_map/ppermute | solution.py:120
  104.7 13.2 %collective-permute-start.13 = (bf16[256,1024]{1,0:T(8,128)(2,1)S(1)}, bf16[256,1024]{1,0:T(8,128)(2,1)S(1)}, u32[]{:S(2)}, u32[]{:S(2)}) collective-permute-start(bf16[256,1024]{1,0:T(8,128)(2,1)S(1)} %collective-permute-done.11), channel_id=1, source_target_pairs={{0,120},{8,0},{16,8},{24,16},{32,24},{40,32},{48,40},{56,48},{64,5... | collective-permute-start | bytes 1572872 | tf_op jit(solution)/shard_map/ppermute | solution.py:125
  112.4 12.5 %collective-permute-start.14 = (bf16[256,1024]{1,0:T(8,128)(2,1)S(1)}, bf16[256,1024]{1,0:T(8,128)(2,1)S(1)}, u32[]{:S(2)}, u32[]{:S(2)}) collective-permute-start(bf16[256,1024]{1,0:T(8,128)(2,1)S(1)} %collective-permute-done.12), channel_id=1, source_target_pairs={{0,8},{8,16},{16,24},{24,32},{32,40},{40,48},{48,56},{56,64},{64,7... | collective-permute-start | bytes 1572872 | tf_op jit(solution)/shard_map/ppermute | solution.py:120
  369.3 35.9 %all-to-all-start.1 = ((bf16[16,2,168,168]{3,1,2,0:T(2,128)(2,1)}), bf16[16,2,168,168]{3,1,2,0:T(2,128)(2,1)S(1)}, u32[]{:S(2)}, u32[]{:S(2)}) async-start(bf16[16,2,168,168]{3,1,2,0:T(2,128)(2,1)} %copy.17), calls=%async_computation.1 | async-start | bytes 5505024 | tf_op jit(solution)/shard_map/all_to_all | solution.py:143
  373.0 92.6 %reduce-scatter.4.cloned.1.call-start = ((), (), s32[]{:S(2)}) async-start(), calls=%async_computation.3 | async-start | bytes 589824
  422.0 45.2 %copy-start.1 = (bf16[16,1681]{1,0:T(8,128)(2,1)S(1)}, bf16[16,1681]{1,0:T(8,128)(2,1)}, u32[]{:S(2)}) copy-start(bf16[16,1681]{1,0:T(8,128)(2,1)} %param.15) | copy-start | bytes 161380
  422.3 4.3 collective-permute-start.15
  424.9 6.0 %collective-permute-start.16 = (bf16[20,1024]{1,0:T(8,128)(2,1)S(1)}, bf16[20,1024]{1,0:T(8,128)(2,1)S(1)}, u32[]{:S(2)}, u32[]{:S(2)}) collective-permute-start(bf16[20,1024]{1,0:T(8,128)(2,1)S(1)} %get-tuple-element.172), channel_id=1, source_target_pairs={{8,0},{16,8},{24,16},{32,24},{40,32},{48,40},{56,48},{64,56},{72,6... | collective-permute-start | bytes 122888 | tf_op jit(solution)/shard_map/ppermute | solution.py:16
Sparse Core Ops, SparseCore 0:
  432.3 33.2 reduce-scatter.3
